TPU v7x, 256 devices: a whole 4x4x8 slice. The times are simulated.
256 devices in a mesh: neuron: 64 (over z, x_hi, y), tm: 4 (over x_lo, core).
Axes of the slice: x: 4 (x_hi: 2, x_lo: 2; x = x_hi * 2 + x_lo), y: 4, z: 8, core: 2. Of those that a mesh axis runs over, the one named last changes fastest.
Arguments:
- data: bfloat16 [8192, 8192], P('neuron', 'tm'), may hold values from 0 to 2
- behaviour: bfloat16 [512, 8192], P('neuron', 'tm'), may hold values from 0 to 2
- motifs: bfloat16 [32, 8192, 128], P('tm', 'neuron'), may hold values from 0 to 2
- behav_motifs: bfloat16 [32, 512, 128], P('tm', 'neuron'), may hold values from 0 to 2
- activations: bfloat16 [128, 8192], P(None, 'tm'), may hold values from 0 to 2
Outputs:
- new_motifs: bfloat16 [32, 8192, 128], P('tm', 'neuron')
- new_behav_motifs: bfloat16 [32, 512, 128], P('tm', 'neuron')
- new_activations: bfloat16 [128, 8192], P(None, 'tm')
All inputs are finite; a program needn't handle non-finite values.
Results may differ from a plain program's by a relative error of at most 0.0034.
Values may be sent and summed in bfloat16 or wider, within the bound.
No kernel may reach another device: no remote copies, remote signals or barrier semaphores. Data moves between devices by JAX's collectives and lax.ppermute only.
A program may use at most 64 MiB of HBM per device.

v0:
```python
import math

import jax
import jax.numpy as jnp
from jax import lax
from jax.sharding import PartitionSpec as P

behaviour_weight = 2.0


def passed_along(shard, axis, by):
    peers = lax.axis_size(axis)
    pairs = [(i, i + by) for i in range(peers) if 0 <= i + by < peers]
    return lax.ppermute(shard, axis, pairs)


def local(data, behaviour, motifs, behav_motifs, activations):
    lags_here, neurons_here, width = motifs.shape
    features_here = behaviour.shape[0]
    frames = activations.shape[1]
    lag_count = lags_here * lax.axis_size("tm")
    all_frames = frames * lax.axis_size("tm")
    all_neurons = neurons_here * lax.axis_size("neuron")
    all_features = features_here * lax.axis_size("neuron")
    scale = 1.0 / (lag_count * width)
    rate_motif = 0.5 * lag_count * width / math.sqrt(all_frames)
    rate_active = 0.5 * lag_count * width / math.sqrt(lag_count * (all_neurons + 4 * all_features))
    rim = lag_count - 1
    earlier = passed_along(activations[:, frames - rim :], "tm", 1)
    extended = jnp.concatenate([earlier, activations], axis=1)

    def window(lag):
        return lax.dynamic_slice_in_dim(extended, rim - lag, frames, 1)

    zero_pair = (
        jnp.zeros((neurons_here, frames), jnp.float32),
        jnp.zeros((features_here, frames), jnp.float32),
    )
    back_start = jnp.zeros((width, rim + frames), jnp.float32)
    gathered = (
        lax.all_gather(motifs, "tm", axis=0, tiled=True),
        lax.all_gather(behav_motifs, "tm", axis=0, tiled=True),
    )

    def one_lag(index, acc):
        win = window(0 + index)
        neuron_rows = lax.dynamic_index_in_dim(gathered[0], index, 0, keepdims=False)
        feature_rows = lax.dynamic_index_in_dim(gathered[1], index, 0, keepdims=False)
        return (
            acc[0] + jnp.dot(neuron_rows, win, preferred_element_type=jnp.float32),
            acc[1] + jnp.dot(feature_rows, win, preferred_element_type=jnp.float32),
        )

    recon_x, recon_b = lax.fori_loop(0, gathered[0].shape[0], one_lag, zero_pair)
    resid_x = (data.astype(jnp.float32) - scale * recon_x).astype(jnp.bfloat16)
    resid_b = (behaviour_weight * (behaviour.astype(jnp.float32) - scale * recon_b)).astype(
        jnp.bfloat16
    )

    def one_lag(index, acc):
        lag = 0 + index
        neuron_rows = lax.dynamic_index_in_dim(gathered[0], index, 0, keepdims=False)
        feature_rows = lax.dynamic_index_in_dim(gathered[1], index, 0, keepdims=False)
        back = lax.dot_general(
            neuron_rows, resid_x, (((0,), (0,)), ((), ())), preferred_element_type=jnp.float32
        )
        back = back + lax.dot_general(
            feature_rows, resid_b, (((0,), (0,)), ((), ())), preferred_element_type=jnp.float32
        )
        place = rim - lag
        current = lax.dynamic_slice_in_dim(acc, place, frames, 1)
        return lax.dynamic_update_slice_in_dim(acc, current + back, place, 1)

    extended_back = lax.fori_loop(0, gathered[0].shape[0], one_lag, back_start)

    def one_lag(index):
        win = window(index)
        neuron_part = lax.dot_general(
            resid_x, win, (((1,), (1,)), ((), ())), preferred_element_type=jnp.float32
        )
        feature_part = lax.dot_general(
            resid_b, win, (((1,), (1,)), ((), ())), preferred_element_type=jnp.float32
        )
        return -scale * jnp.concatenate([neuron_part, feature_part], axis=0)

    gradients = lax.psum_scatter(
        lax.map(one_lag, jnp.arange(lags_here * lax.axis_size("tm"), dtype=jnp.int32)),
        "tm",
        scatter_dimension=0,
        tiled=True,
    )
    grad_motif = gradients[:, :neurons_here]
    grad_behav = gradients[:, neurons_here:]
    new_motifs = jnp.maximum(motifs.astype(jnp.float32) - rate_motif * grad_motif, 0.0).astype(
        jnp.bfloat16
    )
    new_behav = jnp.maximum(behav_motifs.astype(jnp.float32) - rate_motif * grad_behav, 0.0).astype(
        jnp.bfloat16
    )
    spilled = extended_back[:, :rim]
    from_next = passed_along(spilled, "tm", -1)
    own_part = extended_back[:, rim:]
    own_part = own_part.at[:, frames - rim :].add(from_next)
    partial_grad = -scale * own_part
    grad_active = lax.psum(partial_grad, "neuron")
    new_active = jnp.maximum(
        activations.astype(jnp.float32) - rate_active * grad_active, 0.0
    ).astype(jnp.bfloat16)
    return (new_motifs, new_behav, new_active)


def solution(mesh):
    placed = (
        P("neuron", "tm"),
        P("neuron", "tm"),
        P("tm", "neuron", None),
        P("tm", "neuron", None),
        P(None, "tm"),
    )
    return jax.shard_map(
        local,
        mesh=mesh,
        in_specs=placed,
        out_specs=(P("tm", "neuron", None), P("tm", "neuron", None), P(None, "tm")),
        check_vma=False,
    )
```

profile of v0, /device:TPU:1, one launch (start us, length us, event | category | flops | bytes accessed | tf_op | source)
XLA Modules:
  0.0 979.0 jit_solution(6103202162167118137)
XLA Ops:
  8.8 4.5 collective-permute-start
  13.3 5.3 all_gather.7
  19.8 17.4 %all-gather.2.cloned.1.call-done = bf16[32,128,128]{2,1,0:T(8,128)(2,1)} async-done(((bf16[8,128,128]{2,1,0:T(8,128)(2,1)}), bf16[32,128,128]{2,1,0:T(8,128)(2,1)}) %all-gather.2.cloned.1.call-update) | async-done | bytes 1048592 | tf_op jit(solution)/shard_map/all_gather | solution.py:41
  37.2 54.8 %while.48 = (s32[]{:T(128)}, f32[128,2048]{1,0:T(8,128)S(1)}, f32[8,2048]{1,0:T(8,128)S(1)}, bf16[32,128,128]{2,1,0:T(8,128)(2,1)}, bf16[128,2079]{1,0:T(8,128)(...) while((s32[]{:T(128)}, f32[128,2048]{1,0:T(8,128)S(1)}, ...), condition=%wide.region_1.2_spmd.clone, body=%wide.region_0.1_spmd.clone.sunk | while | flops 71860232 | bytes 3312298 | solution.py:54
  92.8 134.5 %while.47 = (s32[]{:T(128)}, f32[128,2079]{1,0:T(8,128)S(1)}, bf16[32,128,128]{2,1,0:T(8,128)(2,1)}, bf16[128,2048]{1,0:T(8,128)(2,1)S(1)}, bf16[32,8,128]{2,1,0...) while((s32[]{:T(128)}, f32[128,2079]{1,0:T(8,128)S(1)}, ...), condition=%wide.region_6.7_spmd, body=%wide.region_5.6_spmd.sunk | while | flops 71827456 | bytes 6883999 | solution.py:74
  94.3 2.7 dynamic_update_slice.21
  98.6 2.7 dynamic_update_slice.21
  102.8 2.7 dynamic_update_slice.21
  107.0 2.7 dynamic_update_slice.21
  115.5 2.7 dynamic_update_slice.21
  124.0 2.7 dynamic_update_slice.21
  132.5 2.7 dynamic_update_slice.21
  140.9 2.7 dynamic_update_slice.21
  149.4 2.7 dynamic_update_slice.21
  157.9 2.7 dynamic_update_slice.21
  166.3 2.7 dynamic_update_slice.21
  196.0 2.7 dynamic_update_slice.21
  204.5 2.7 dynamic_update_slice.21
  212.9 2.7 dynamic_update_slice.21
  221.4 2.7 dynamic_update_slice.21
  229.6 3.3 collective-permute-done.1
  234.7 105.0 %while.46 = (s32[]{:T(128)}, f32[32,136,128]{2,1,0:T(8,128)}, s32[32]{0:T(128)S(1)}, bf16[128,2079]{1,0:T(8,128)(2,1)S(1)}, bf16[128,2048]{1,0:T(8,128)(2,1)S(1)...) while((s32[]{:T(128)}, f32[32,136,128]{2,1,0:T(8,128)}, ...), condition=%wide.region_3.4_spmd, body=%wide.region_2.3_spmd.sunk | while | flops 71337992 | bytes 1815207 | solution.py:87
  339.8 553.3 %all-reduce.2.cloned.1.call-done = f32[128,2048]{1,0:T(8,128)} async-done(((f32[128,2048]{1,0:T(8,128)}), f32[128,2048]{1,0:T(8,128)}) %all-reduce.2.cloned.1.call-update) | async-done | bytes 1048592 | tf_op jit(solution)/shard_map/psum | solution.py:105
  895.3 73.9 %reduce-scatter.2.cloned.1.call-done = f32[8,136,128]{2,1,0:T(8,128)} async-done(((f32[32,136,128]{2,1,0:T(8,128)}), f32[8,136,128]{2,1,0:T(8,128)}) %reduce-scatter.2.cloned.1.call-update) | async-done | bytes 557072 | tf_op jit(solution)/shard_map/reduce_scatter | solution.py:86
  (308 shorter events, 223.2 us)
Async XLA Ops:
  7.2 30.0 %all-gather.2.cloned.1.call-start = ((), (), s32[]{:S(2)}) async-start(), calls=%async_computation.1 | async-start | bytes 1310720 | tf_op jit(solution)/shard_map/all_gather | solution.py:41
  7.9 885.2 %all-reduce.2.cloned.1.call-start = ((), (), s32[]{:S(2)}) async-start(), calls=%async_computation.3 | async-start | bytes 2097152 | tf_op jit(solution)/shard_map/psum | solution.py:105
  8.8 9.8 collective-permute-start
  37.2 54.8 %copy-start.2 = (bf16[128,2048]{1,0:T(8,128)(2,1)S(1)}, bf16[128,2048]{1,0:T(8,128)(2,1)}, u32[]{:S(2)}) copy-start(bf16[128,2048]{1,0:T(8,128)(2,1)} %param.13) | copy-start | bytes 1572868
  92.0 0.8 copy-start.4
  227.4 5.6 collective-permute-start.1
  234.6 734.6 %reduce-scatter.2.cloned.1.call-start = ((), (), s32[]{:S(2)}) async-start(), calls=%async_computation.2 | async-start | bytes 2785280 | tf_op jit(solution)/shard_map/reduce_scatter | solution.py:86
  339.7 553.4 %copy-start = (bf16[128,2048]{1,0:T(8,128)(2,1)S(1)}, bf16[128,2048]{1,0:T(8,128)(2,1)}, u32[]{:S(2)}) copy-start(bf16[128,2048]{1,0:T(8,128)(2,1)} %param.17) | copy-start | bytes 1572868
  339.8 629.5 %copy-start.1 = (bf16[8,128,128]{2,1,0:T(8,128)(2,1)S(1)}, bf16[8,128,128]{2,1,0:T(8,128)(2,1)}, u32[]{:S(2)}) copy-start(bf16[8,128,128]{2,1,0:T(8,128)(2,1)} %param.15) | copy-start | bytes 786436
  339.8 631.3 %copy-start.3 = (bf16[8,8,128]{2,1,0:T(8,128)(2,1)S(1)}, bf16[8,8,128]{2,1,0:T(8,128)(2,1)}, u32[]{:S(2)}) copy-start(bf16[8,8,128]{2,1,0:T(8,128)(2,1)} %param.16) | copy-start | bytes 49156
Sparse Core Ops, SparseCore 0:
  9.8 27.3 all-gather.1
  234.8 658.3 all-reduce.1
  895.7 73.4 reduce-scatter.1
where the time goes:
time: 984 us; the launch traced here: 979 us
  waiting for transfers between devices  649 us (66%)
  matrix products  126 us (13%)
  local copies, waits for them, and re-layouts  107 us (11%)
  loops' own time  43.4 us (4%)
  other arithmetic  28.5 us (3%)
  between operations  13.9 us (1%)
    psum x1, waiting for transfers between devices, local(): grad_active = lax.psum(partial_grad, 'neuron')  553 us
    dynamic_update_slice x32, local copies, waits for them, and re-layouts, one_lag(): return lax.dynamic_update_slice_in_dim(acc, current + back, place, 1)  85.9 us
    reduce_scatter x1, waiting for transfers between devices, local(): lax.psum_scatter(lax.map(one_lag, jnp.arange(lags_here * lax.axis_size('t...  73.9 us
    dot_general x32, matrix products, one_lag(): jnp.dot(neuron_rows, win, preferred_element_type=jnp.float32)  43.7 us
    another operation x1, loops' own time, local(): lax.map(one_lag, jnp.arange(lags_here * lax.axis_size('tm'), dtype=jnp.in...  41.9 us
    dot_general x32, matrix products, one_lag(): lax.dot_general(neuron_rows, resid_x, (((0,), (0,)), ((), ())), preferred...  34.5 us
    dynamic_update_slice x32, other arithmetic, local(): lax.map(one_lag, jnp.arange(lags_here * lax.axis_size('tm'), dtype=jnp.in...  20.6 us
  transfers between devices with their start and end apart: 5, of which 4 were waited for; matrix products, arithmetic and copies ran while one was open for 7% of the time, Pallas kernels for 0%

commit v1 on v0

v1 whole, which is shorter than its diff:
```python
import functools
import math

import jax
import jax.numpy as jnp
from jax import lax
from jax.experimental import pallas as pl
from jax.experimental.pallas import tpu as pltpu
from jax.sharding import PartitionSpec as P


behaviour_weight = 2.0
lane = 128
group = 4
deep, wide = 16, 4
patch = 32
f32 = jnp.float32
bf16 = jnp.bfloat16
VMEM = pl.BlockSpec(memory_space=pltpu.VMEM)


def along(shard, by):
    pairs = [(i, i + by) for i in range(4) if 0 <= i + by < 4]
    return lax.ppermute(shard, "tm", pairs)


def crossed(shard, mask):
    return lax.ppermute(shard, "tm", [(i, i ^ mask) for i in range(4)])


def around(shard, by):
    pairs = [(i * wide + y, i * wide + (y + by) % wide) for i in range(deep) for y in range(wide)]
    return lax.ppermute(shard, "neuron", pairs)


def exchanged(blocks):
    groups = [[i * wide + y for i in range(deep)] for y in range(wide)]
    return lax.all_to_all(blocks, "neuron", 0, 0, axis_index_groups=groups, tiled=True)


def place():
    me = lax.axis_index("neuron")
    return me // wide, me % wide


def moved(x, by):
    by = by % x.shape[1]
    return x if by == 0 else pltpu.roll(x, x.shape[1] - by, 1)


def tiles(width, step):
    at = 0
    while at < width:
        size = min(step, width - at)
        yield at, size
        at += size


def shift_activations(earlier_ref, active_ref, later_ref, stack_ref, ext_ref):
    motifs, frames = active_ref.shape
    width = stack_ref.shape[1]
    steps = stack_ref.shape[0] // motifs
    rows = 16
    ext_ref[:, :lane] = earlier_ref[...]
    ext_ref[:, lane : lane + frames] = active_ref[...]
    ext_ref[:, lane + frames :] = later_ref[...]

    def chunk(i, carry):
        at = pl.multiple_of(i * rows, rows)
        block = ext_ref[pl.ds(at, rows), :]
        for a in range(steps):
            by = lane - (group - 1) - group * a
            stack_ref[pl.ds(pl.multiple_of(a * motifs + at, rows), rows), :] = moved(block, by)[:, :width]
        return carry

    lax.fori_loop(0, motifs // rows, chunk, 0)


def forward_backward(scale, frames, *refs):
    stack_ref, data_ref, data_halo_ref, behav_ref, behav_halo_ref = refs[:5]
    w_parts, v_parts = refs[5:9], refs[9:13]
    grad_refs, resid_ref = refs[13:17], refs[17]
    w_ref, v_ref, out_ref, back_ref, few_ref, sum_ref = refs[18:]
    lags, neurons, motifs = w_ref.shape
    features = v_ref.shape[1]
    steps = lags // group
    width = frames + lane
    mine = lax.axis_index("tm")
    _, y = place()
    part = lags // 4
    for p in range(4):
        from_device = mine ^ p
        w_ref[pl.ds(from_device * part, part)] = w_parts[p][...]
        v_ref[pl.ds(from_device * part, part)] = v_parts[p][...]

    rows_w = [jnp.concatenate([w_ref[group * a + b] for a in range(steps)], axis=1) for b in range(group)]
    rows_v = jnp.concatenate(
        [v_ref[group * a : group * (a + 1)].reshape(group * features, motifs) for a in range(steps)], axis=1
    )
    left = jnp.concatenate(rows_w + [rows_v], axis=0)
    for at, size in tiles(width, 256):
        out_ref[:, at : at + size] = jnp.dot(left, stack_ref[:, at : at + size], preferred_element_type=f32)

    valid = mine < 3
    rows = 8

    def residual(i, carry):
        at = pl.multiple_of(i * rows, rows)
        total = None
        for b in range(group):
            term = moved(out_ref[pl.ds(pl.multiple_of(b * neurons + at, rows), rows), :], group - 1 - b)
            total = term if total is None else total + term
        own = data_ref[pl.ds(at, rows), :].astype(f32) - scale * total[:, :frames]
        halo = data_halo_ref[pl.ds(at, rows), :].astype(f32) - scale * total[:, frames:]
        halo = jnp.where(valid, halo, 0.0)
        resid_ref[pl.ds(at, rows), :] = jnp.concatenate([own, halo], axis=1).astype(bf16)
        return carry

    lax.fori_loop(0, neurons // rows, residual, 0)
    total = None
    for b in range(group):
        first = group * neurons + b * features
        term = moved(out_ref[first : first + features, :], group - 1 - b)
        total = term if total is None else total + term
    own = behaviour_weight * (behav_ref[...].astype(f32) - scale * total[:, :frames])
    halo = behaviour_weight * (behav_halo_ref[...].astype(f32) - scale * total[:, frames:])
    halo = jnp.where(valid, halo, 0.0)
    resid_few = jnp.concatenate([own, halo], axis=1).astype(bf16)
    resid_ref[neurons:, :] = resid_few

    rows = 16

    def chunk(i, carry):
        at = pl.multiple_of(i * rows, rows)
        block = resid_ref[pl.ds(at, rows), :]
        for a in range(steps):
            back_ref[pl.ds(pl.multiple_of(a * neurons + at, rows), rows), :] = moved(block, group * a)
        return carry

    lax.fori_loop(0, neurons // rows, chunk, 0)
    few = resid_few.astype(f32)
    for l in range(0, lags, 2):
        pair = jnp.concatenate([moved(few, l)[:, :frames], moved(few, l + 1)[:, :frames]], axis=0)
        few_ref[l * features : (l + 2) * features, :] = pair.astype(bf16)

    left = jnp.concatenate(
        [jnp.concatenate([w_ref[group * a + b].T for a in range(steps)], axis=1) for b in range(group)], axis=0
    )
    for at, size in tiles(width, 256):
        out_ref[: group * motifs, at : at + size] = jnp.dot(
            left, back_ref[:, at : at + size], preferred_element_type=f32
        )
    left = v_ref[...].reshape(lags * features, motifs).T
    for at, size in tiles(frames, 256):
        total = jnp.dot(left, few_ref[:, at : at + size], preferred_element_type=f32)
        for b in range(group):
            reach = out_ref[b * motifs : (b + 1) * motifs, at : at + size + lane]
            total = total + moved(reach, b)[:, :size]
        for i in range(motifs // patch):
            for j in range(size // lane):
                sum_ref[i * (frames // lane) + at // lane + j] = total[
                    patch * i : patch * (i + 1), lane * j : lane * (j + 1)
                ]
    for r in range(wide):
        peer = (y + r) % wide
        grad_refs[r][...] = sum_ref[pl.ds(peer * deep, deep)].astype(grad_refs[r].dtype)


def motif_gradients(frames, motifs, stack_ref, resid_ref, keep_ref, relay_ref, send_ref, left_ref):
    features = keep_ref.shape[1] - 128
    neurons = resid_ref.shape[0] - features
    steps = stack_ref.shape[0] // motifs
    width = frames + lane
    rows = 16
    mask = lax.broadcasted_iota(jnp.int32, (rows, width), 1) < frames

    def chunk(i, carry):
        at = pl.multiple_of(i * rows, rows)
        block = jnp.where(mask, resid_ref[pl.ds(at, rows), :].astype(f32), 0.0)
        for b in range(group):
            shifted = moved(block, b - (group - 1)).astype(bf16)
            left_ref[pl.ds(pl.multiple_of(b * neurons + at, rows), rows), :] = shifted
        return carry

    lax.fori_loop(0, neurons // rows, chunk, 0)
    block = jnp.where(mask[:features], resid_ref[neurons:, :].astype(f32), 0.0)
    left_ref[group * neurons :, :] = jnp.concatenate(
        [moved(block, b - (group - 1)) for b in range(group)], axis=0
    ).astype(bf16)
    mine = lax.axis_index("tm")
    span = steps * motifs // 4
    for p in (3, 1, 2, 0):
        first = pl.multiple_of((mine ^ p) * span, span)
        result = lax.dot_general(
            left_ref[...], stack_ref[pl.ds(first, span), :], (((1,), (1,)), ((), ())), preferred_element_type=f32
        )
        for a in range(span // motifs):
            for b in range(group):
                target = (keep_ref, send_ref.at[0], relay_ref, send_ref.at[1])[p]
                l = group * a + b
                cols = slice(a * motifs, (a + 1) * motifs)
                few = group * neurons + b * features
                target[l, :neurons, :] = result[b * neurons : (b + 1) * neurons, cols].astype(target.dtype)
                target[l, neurons:, :] = result[few : few + features, cols].astype(target.dtype)


def sum_around(*refs):
    parts, out_ref = refs[:wide], refs[wide]
    total = parts[0][...]
    for part in parts[1:]:
        total = total + part[...].astype(f32)
    out_ref[...] = total.astype(out_ref.dtype)


def update(factor, active_ref, parts_ref, out_ref):
    i, y = place()
    own = active_ref[pl.ds(pl.multiple_of(y * patch, patch), patch), pl.ds(pl.multiple_of(i * lane, lane), lane)]
    total = jnp.sum(parts_ref[...].astype(f32), axis=0)
    block = jnp.maximum(own.astype(f32) + factor * total, 0.0).astype(bf16)
    for j in range(deep):
        out_ref[j] = block


def join_columns(parts_ref, out_ref):
    for j in range(deep):
        out_ref[:, lane * j : lane * (j + 1)] = parts_ref[j]


def join_rows(*refs):
    parts, out_ref = refs[:wide], refs[wide]
    _, y = place()
    for r in range(wide):
        row = pl.multiple_of((y + wide - r) % wide * patch, patch)
        out_ref[pl.ds(row, patch), :] = parts[r][...]


def call(body, out_shape, scratch, args, flops=0, moves=1 << 20, vmem=8):
    return pl.pallas_call(
        body,
        out_shape=out_shape,
        in_specs=[VMEM] * len(args),
        out_specs=jax.tree.map(lambda _: VMEM, out_shape),
        scratch_shapes=scratch,
        compiler_params=pltpu.CompilerParams(vmem_limit_bytes=vmem << 20),
        cost_estimate=pl.CostEstimate(flops=flops, bytes_accessed=moves, transcendentals=0),
    )(*args)


def local(data, behaviour, motifs, behav_motifs, activations):
    lags_here, neurons, width = motifs.shape
    features = behaviour.shape[0]
    frames = activations.shape[1]
    lags = lags_here * lax.axis_size("tm")
    all_frames = frames * lax.axis_size("tm")
    all_neurons = neurons * lax.axis_size("neuron")
    all_features = features * lax.axis_size("neuron")
    scale = 1.0 / (lags * width)
    rate_motif = 0.5 * lags * width / math.sqrt(all_frames)
    rate_active = 0.5 * lags * width / math.sqrt(lags * (all_neurons + 4 * all_features))
    shape = jax.ShapeDtypeStruct
    steps = lags // group

    w2, v2 = crossed(motifs, 2), crossed(behav_motifs, 2)
    w1, v1 = crossed(motifs, 1), crossed(behav_motifs, 1)
    earlier = along(activations[:, frames - lane :], 1)
    heads = along(
        jnp.concatenate([data[:, :lane], activations[:, :lane], behaviour[:, :lane]], axis=0), -1
    )
    w3, v3 = crossed(w2, 1), crossed(v2, 1)
    stack = call(
        shift_activations,
        shape((steps * width, frames + lane), bf16),
        [pltpu.VMEM((width, frames + 2 * lane), bf16)],
        [earlier, activations, heads[neurons : neurons + width]],
        moves=16 << 20,
        vmem=8,
    )

    grads_and_more = call(
        functools.partial(forward_backward, scale, frames),
        [shape((deep, patch, lane), f32 if r == 0 else bf16) for r in range(wide)]
        + [shape((neurons + features, frames + lane), bf16)],
        [
            pltpu.VMEM((lags, neurons, width), bf16),
            pltpu.VMEM((lags, features, width), bf16),
            pltpu.VMEM((group * (neurons + features), frames + lane), f32),
            pltpu.VMEM((steps * neurons, frames + lane), bf16),
            pltpu.VMEM((lags * features, frames), bf16),
            pltpu.VMEM((deep * wide, patch, lane), f32),
        ],
        [stack, data, heads[:neurons], behaviour, heads[neurons + width :], motifs, w1, w2, w3, behav_motifs, v1, v2, v3],
        flops=4 * lags * (neurons + features) * width * frames,
        moves=4 << 20,
        vmem=30,
    )
    grads, resid = grads_and_more[:wide], grads_and_more[wide]
    around_parts = [grads[0]]
    for r in range(1, wide):
        around_parts.append(around(grads[r], r))

    per_lag = (lags_here, neurons + features, width)
    keep, relay, send = call(
        functools.partial(motif_gradients, frames, width),
        [shape(per_lag, f32), shape(per_lag, f32), shape((2,) + per_lag, f32)],
        [pltpu.VMEM((group * (neurons + features), frames + lane), bf16)],
        [stack, resid],
        flops=2 * lags * (neurons + features) * width * frames,
        moves=4 << 20,
        vmem=20,
    )
    got = crossed(send, 1)

    sums = call(sum_around, shape((deep, patch, lane), bf16), [], around_parts)
    relayed = crossed(relay + got[1], 2)
    blocks = call(
        functools.partial(update, rate_active * scale),
        shape((deep, patch, lane), bf16),
        [],
        [activations, exchanged(sums)],
    )
    strip = call(join_columns, shape((patch, frames), bf16), [], [exchanged(blocks)])
    new_active = call(
        join_rows,
        shape((width, frames), bf16),
        [],
        [strip] + [around(strip, r) for r in range(1, wide)],
    )

    total = keep + got[0] + relayed
    step = rate_motif * scale
    new_motifs = jnp.maximum(motifs.astype(f32) + step * total[:, :neurons], 0.0).astype(bf16)
    new_behav = jnp.maximum(behav_motifs.astype(f32) + step * total[:, neurons:], 0.0).astype(bf16)
    return (new_motifs, new_behav, new_active)


def solution(mesh):
    placed = (
        P("neuron", "tm"),
        P("neuron", "tm"),
        P("tm", "neuron", None),
        P("tm", "neuron", None),
        P(None, "tm"),
    )
    return jax.shard_map(
        local,
        mesh=mesh,
        in_specs=placed,
        out_specs=(P("tm", "neuron", None), P("tm", "neuron", None), P(None, "tm")),
        check_vma=False,
    )
```

time: 984 us -> 95.2 us (0.10)
  the two profiles are of different devices: /device:TPU:1 before, /device:TPU:10 now
where the time goes in v1:
time: 95.2 us; the launch traced here: 94.7 us
  waiting for transfers between devices  29.3 us (31%)
  starting transfers between devices  26.5 us (28%)
  Pallas kernels  17.3 us (18%)
  blocking collectives  13.9 us (15%)
  other arithmetic  3.66 us (4%)
  local copies, waits for them, and re-layouts  3.29 us (3%)
    pallas_call x7, Pallas kernels, call(): pl.pallas_call(body, out_shape=out_shape, in_specs=[VMEM] * len(args), ou...  17.3 us
    all_to_all x1, blocking collectives, exchanged(): lax.all_to_all(blocks, 'neuron', 0, 0, axis_index_groups=groups, tiled=True)  13.9 us
    ppermute x6, waiting for transfers between devices, around(): return lax.ppermute(shard, 'neuron', pairs)  10.4 us
    all_to_all x1, starting transfers between devices, exchanged(): lax.all_to_all(blocks, 'neuron', 0, 0, axis_index_groups=groups, tiled=True)  10.3 us
    all_to_all x1, waiting for transfers between devices, exchanged(): lax.all_to_all(blocks, 'neuron', 0, 0, axis_index_groups=groups, tiled=True)  9.72 us
    ppermute x6, starting transfers between devices, around(): return lax.ppermute(shard, 'neuron', pairs)  9.68 us
    ppermute x8, waiting for transfers between devices, crossed(): return lax.ppermute(shard, 'tm', [(i, i ^ mask) for i in range(4)])  6.02 us
    ppermute x2, starting transfers between devices, along(): return lax.ppermute(shard, 'tm', pairs)  4.47 us
  transfers between devices with their start and end apart: 17, of which 10 were waited for; matrix products, arithmetic and copies ran while one was open for 4% of the time, Pallas kernels for 4%

profile of v1, /device:TPU:10, one launch (start us, length us, event | category | flops | bytes accessed | tf_op | source)
XLA Modules:
  0.0 94.7 jit_solution(14336812473938427099)
XLA Ops:
  3.5 2.6 %collective-permute-start.1 = (bf16[264,128]{1,0:T(8,128)(2,1)S(1)}, bf16[264,128]{1,0:T(8,128)(2,1)S(1)}, u32[]{:S(2)}, u32[]{:S(2)}) collective-permute-start(bf16[264,128]{1,0:T(8,128)(2,1)S(1)} %pad_maximum_fusion), channel_id=1, source_target_pairs={{1,0},{2,1},{3,2},{5,4},{6,5},{7,6},{9,8},{10,9},{11,10},{13,12},{... | collective-permute-start | bytes 202760 | tf_op jit(solution)/shard_map/ppermute | solution.py:24
  6.2 2.8 %collective-permute-done.3.refs_7_ = bf16[8,128,128]{2,1,0:T(8,128)(2,1)S(1)} collective-permute-done((bf16[8,128,128]{2,1,0:T(8,128)(2,1)}, bf16[8,128,128]{2,1,0:T(8,128)(2,1)S(1)}, u32[]{:S(2)}, u32[]{:S(2)}) %collective-permute-start.3) | collective-permute-done | bytes 262176 | tf_op jit(solution)/shard_map/ppermute | solution.py:28
  9.7 3.2 %collective-permute-done.6.refs_11_ = bf16[8,8,128]{2,1,0:T(8,128)(2,1)S(1)} collective-permute-done((bf16[8,8,128]{2,1,0:T(8,128)(2,1)}, bf16[8,8,128]{2,1,0:T(8,128)(2,1)S(1)}, u32[]{:S(2)}, u32[]{:S(2)}) %collective-permute-start.6) | collective-permute-done | bytes 16416 | tf_op jit(solution)/shard_map/ppermute | solution.py:28
  12.9 1.9 %collective-permute-start = (bf16[128,128]{1,0:T(8,128)(2,1)S(1)}, bf16[128,128]{1,0:T(8,128)(2,1)S(1)}, u32[]{:S(2)}, u32[]{:S(2)}) collective-permute-start(bf16[128,128]{1,0:T(8,128)(2,1)S(1)} %get-tuple-element.20), channel_id=1, source_target_pairs={{0,1},{1,2},{2,3},{4,5},{5,6},{6,7},{8,9},{9,10},{10,11},{12,13},{... | collective-permute-start | bytes 98312 | tf_op jit(solution)/shard_map/ppermute | solution.py:24
  15.0 3.2 %collective-permute-done.earlier_ref = bf16[128,128]{1,0:T(8,128)(2,1)S(1)} collective-permute-done((bf16[128,128]{1,0:T(8,128)(2,1)S(1)}, bf16[128,128]{1,0:T(8,128)(2,1)S(1)}, u32[]{:S(2)}, u32[]{:S(2)}) %collective-permute-start) | collective-permute-done | bytes 32800 | tf_op jit(solution)/shard_map/ppermute | solution.py:24
  18.2 1.0 %copy-done = bf16[128,2048]{1,0:T(8,128)(2,1)S(1)} copy-done((bf16[128,2048]{1,0:T(8,128)(2,1)S(1)}, bf16[128,2048]{1,0:T(8,128)(2,1)}, u32[]{:S(2)}) %copy-start) | copy-done | bytes 524312
  19.2 1.8 %shard_map.76.refs_0_.stack_ref = bf16[1024,2176]{1,0:T(8,128)(2,1)S(1)} custom-call(bf16[128,128]{1,0:T(8,128)(2,1)S(1)} %collective-permute-done.earlier_ref, bf16[128,2048]{1,0:T(8,128)(2,1)S(1)} %copy-done, bf16[128,128]{1,0:T(8,128)(2,1)S(1)} %get-tuple-element.22.later_ref), custom_call_target="tpu_custom_call" | custom-call | bytes 16777216 | tf_op jit(solution)/shard_map/pallas_call | solution.py:238
  21.1 10.0 %shard_map.77 = (f32[16,32,128]{2,1,0:T(8,128)S(1)}, bf16[16,32,128]{2,1,0:T(8,128)(2,1)S(1)}, bf16[16,32,128]{2,1,0:T(8,128)(2,1)S(1)}, bf16[16,32,128]{2,1,0:T(8,128)(2,1)S(1)}, bf16[136,2176]{1,0:T(8,128)(2,1)S(1)}) custom-call(bf16[1024,2176]{1,0:T(8,128)(2,1)S(1)} %shard_map.76.refs_0_.stack_ref, bf16[128,2048]{1,0:T(8,128)(2,1)S(1)} %copy-done.4, ...), custom_call_target="tpu_custom_call" | custom-call | flops 4563402752 | bytes 4194304 | tf_op jit(solution)/shard_map/pallas_call | solution.py:238
  31.1 3.8 %shard_map.78 = (f32[8,136,128]{2,1,0:T(8,128)S(1)}, f32[8,136,128]{2,1,0:T(8,128)S(1)}, f32[2,8,136,128]{3,2,1,0:T(8,128)S(1)}) custom-call(bf16[1024,2176]{1,0:T(8,128)(2,1)S(1)} %shard_map.76.refs_0_.stack_ref, bf16[136,2176]{1,0:T(8,128)(2,1)S(1)} %get-tuple-element.11.resid_ref), custom_call_target="tpu_custom_call" | custom-call | flops 2281701376 | bytes 4194304 | tf_op jit(solution)/shard_map/pallas_call | solution.py:238
  35.1 1.8 %collective-permute-start.10 = (bf16[16,32,128]{2,1,0:T(8,128)(2,1)S(1)}, bf16[16,32,128]{2,1,0:T(8,128)(2,1)S(1)}, u32[]{:S(2)}, u32[]{:S(2)}) collective-permute-start(bf16[16,32,128]{2,1,0:T(8,128)(2,1)S(1)} %get-tuple-element.16), channel_id=1, source_target_pairs={{0,4},{4,8},{8,12},{12,0},{16,20},{20,24},{24,28},{28,16},{32,36},... | collective-permute-start | bytes 393224 | tf_op jit(solution)/shard_map/ppermute | solution.py:33
  36.9 0.9 collective-permute-start.11
  37.8 2.4 %collective-permute-start.12 = (bf16[16,32,128]{2,1,0:T(8,128)(2,1)S(1)}, bf16[16,32,128]{2,1,0:T(8,128)(2,1)S(1)}, u32[]{:S(2)}, u32[]{:S(2)}) collective-permute-start(bf16[16,32,128]{2,1,0:T(8,128)(2,1)S(1)} %get-tuple-element.18), channel_id=1, source_target_pairs={{0,12},{4,0},{8,4},{12,8},{16,28},{20,16},{24,20},{28,24},{32,44},... | collective-permute-start | bytes 393224 | tf_op jit(solution)/shard_map/ppermute | solution.py:33
  41.2 3.6 %collective-permute-done.11.refs_2_ = bf16[16,32,128]{2,1,0:T(8,128)(2,1)S(1)} collective-permute-done((bf16[16,32,128]{2,1,0:T(8,128)(2,1)S(1)}, bf16[16,32,128]{2,1,0:T(8,128)(2,1)S(1)}, u32[]{:S(2)}, u32[]{:S(2)}) %collective-permute-start.11) | collective-permute-done | bytes 131104 | tf_op jit(solution)/shard_map/ppermute | solution.py:33
  44.8 1.0 %collective-permute-done.12.refs_3_ = bf16[16,32,128]{2,1,0:T(8,128)(2,1)S(1)} collective-permute-done((bf16[16,32,128]{2,1,0:T(8,128)(2,1)S(1)}, bf16[16,32,128]{2,1,0:T(8,128)(2,1)S(1)}, u32[]{:S(2)}, u32[]{:S(2)}) %collective-permute-start.12) | collective-permute-done | bytes 131104 | tf_op jit(solution)/shard_map/ppermute | solution.py:33
  46.5 10.3 %all-to-all-start = ((bf16[16,32,128]{2,1,0:T(8,128)(2,1)}), bf16[16,32,128]{2,1,0:T(8,128)(2,1)S(1)}, u32[]{:S(2)}, u32[]{:S(2)}) async-start(bf16[16,32,128]{2,1,0:T(8,128)(2,1)} %shard_map.79), calls=%async_computation | async-start | bytes 262144 | tf_op jit(solution)/shard_map/all_to_all | solution.py:38
  56.8 1.1 %fusion = f32[8,136,128]{2,1,0:T(8,128)S(1)} fusion(f32[8,136,128]{2,1,0:T(8,128)S(1)} %get-tuple-element.14, f32[2,8,136,128]{3,2,1,0:T(8,128)} %collective-permute-done.8), kind=kLoop, calls=%fused_computation.1 | loop fusion | flops 139264 | bytes 1671168 | tf_op jit(solution)/shard_map/add | solution.py:314
  58.3 9.7 %all-to-all-done.parts_ref = bf16[16,32,128]{2,1,0:T(8,128)(2,1)S(1)} async-done(((bf16[16,32,128]{2,1,0:T(8,128)(2,1)}), bf16[16,32,128]{2,1,0:T(8,128)(2,1)S(1)}, u32[]{:S(2)}, u32[]{:S(2)}) %all-to-all-start) | async-done | bytes 131104 | tf_op jit(solution)/shard_map/all_to_all | solution.py:38
  68.1 13.9 %all_to_all.10.parts_ref = bf16[16,32,128]{2,1,0:T(8,128)(2,1)S(1)} all-to-all(bf16[16,32,128]{2,1,0:T(8,128)(2,1)S(1)} %shard_map.80), channel_id=1, replica_groups={{0,16,32,48,64,80,96,112,128,144,160,176,192,208,224,240},{4,20,36,52,6..., dimensions={0} | all-to-all | bytes 262144 | tf_op jit(solution)/shard_map/all_to_all | solution.py:38
  81.9 1.5 %collective-permute-start.13 = (bf16[32,2048]{1,0:T(8,128)(2,1)S(1)}, bf16[32,2048]{1,0:T(8,128)(2,1)S(1)}, u32[]{:S(2)}, u32[]{:S(2)}) collective-permute-start(bf16[32,2048]{1,0:T(8,128)(2,1)S(1)} %shard_map.81.refs_0_), channel_id=1, source_target_pairs={{0,4},{4,8},{8,12},{12,0},{16,20},{20,24},{24,28},{28,16},{32,36},... | collective-permute-start | bytes 393224 | tf_op jit(solution)/shard_map/ppermute | solution.py:33
  83.4 1.6 %collective-permute-start.14 = (bf16[32,2048]{1,0:T(8,128)(2,1)S(1)}, bf16[32,2048]{1,0:T(8,128)(2,1)S(1)}, u32[]{:S(2)}, u32[]{:S(2)}) collective-permute-start(bf16[32,2048]{1,0:T(8,128)(2,1)S(1)} %shard_map.81.refs_0_), channel_id=1, source_target_pairs={{0,8},{4,12},{8,0},{12,4},{16,24},{20,28},{24,16},{28,20},{32,40},... | collective-permute-start | bytes 393224 | tf_op jit(solution)/shard_map/ppermute | solution.py:33
  85.0 1.5 %collective-permute-start.15 = (bf16[32,2048]{1,0:T(8,128)(2,1)S(1)}, bf16[32,2048]{1,0:T(8,128)(2,1)S(1)}, u32[]{:S(2)}, u32[]{:S(2)}) collective-permute-start(bf16[32,2048]{1,0:T(8,128)(2,1)S(1)} %shard_map.81.refs_0_), channel_id=1, source_target_pairs={{0,12},{4,0},{8,4},{12,8},{16,28},{20,16},{24,20},{28,24},{32,44},... | collective-permute-start | bytes 393224 | tf_op jit(solution)/shard_map/ppermute | solution.py:33
  87.0 3.0 %collective-permute-done.14.refs_2_ = bf16[32,2048]{1,0:T(8,128)(2,1)S(1)} collective-permute-done((bf16[32,2048]{1,0:T(8,128)(2,1)S(1)}, bf16[32,2048]{1,0:T(8,128)(2,1)S(1)}, u32[]{:S(2)}, u32[]{:S(2)}) %collective-permute-start.14) | collective-permute-done | bytes 131104 | tf_op jit(solution)/shard_map/ppermute | solution.py:33
  90.0 1.3 %collective-permute-done.15.refs_3_ = bf16[32,2048]{1,0:T(8,128)(2,1)S(1)} collective-permute-done((bf16[32,2048]{1,0:T(8,128)(2,1)S(1)}, bf16[32,2048]{1,0:T(8,128)(2,1)S(1)}, u32[]{:S(2)}, u32[]{:S(2)}) %collective-permute-start.15) | collective-permute-done | bytes 131104 | tf_op jit(solution)/shard_map/ppermute | solution.py:33
  92.1 1.1 %fusion.2 = f32[8,136,128]{2,1,0:T(8,128)S(1)} fusion(f32[8,136,128]{2,1,0:T(8,128)S(1)} %collective-permute-done.9, f32[8,136,128]{2,1,0:T(8,128)S(1)} %get-tuple-element.12, f32[2,8,136,128]{3,2,1,0:T(8,128)} %collective-permute-done.8), kind=kLoop, calls=%fused_computation.4 | loop fusion | flops 278528 | bytes 2228224 | tf_op jit(solution)/shard_map/add | solution.py:329
  (40 shorter events, 8.8 us)
Async XLA Ops:
  0.6 8.3 %collective-permute-start.3 = (bf16[8,128,128]{2,1,0:T(8,128)(2,1)}, bf16[8,128,128]{2,1,0:T(8,128)(2,1)S(1)}, u32[]{:S(2)}, u32[]{:S(2)}) collective-permute-start(bf16[8,128,128]{2,1,0:T(8,128)(2,1)} %refs_5_.1), channel_id=1, source_target_pairs={{0,2},{1,3},{2,0},{3,1},{4,6},{5,7},{6,4},{7,5},{8,10},{9,11},{10,... | collective-permute-start | bytes 786440 | tf_op jit(solution)/shard_map/ppermute | solution.py:28
  3.5 11.4 %collective-permute-start.1 = (bf16[264,128]{1,0:T(8,128)(2,1)S(1)}, bf16[264,128]{1,0:T(8,128)(2,1)S(1)}, u32[]{:S(2)}, u32[]{:S(2)}) collective-permute-start(bf16[264,128]{1,0:T(8,128)(2,1)S(1)} %pad_maximum_fusion), channel_id=1, source_target_pairs={{1,0},{2,1},{3,2},{5,4},{6,5},{7,6},{9,8},{10,9},{11,10},{13,12},{... | collective-permute-start | bytes 202760 | tf_op jit(solution)/shard_map/ppermute | solution.py:24
  6.1 15.0 %collective-permute-start.2 = (bf16[8,128,128]{2,1,0:T(8,128)(2,1)}, bf16[8,128,128]{2,1,0:T(8,128)(2,1)S(1)}, u32[]{:S(2)}, u32[]{:S(2)}) collective-permute-start(bf16[8,128,128]{2,1,0:T(8,128)(2,1)} %refs_5_.1), channel_id=1, source_target_pairs={{0,1},{1,0},{2,3},{3,2},{4,5},{5,4},{6,7},{7,6},{8,9},{9,8},{10,11... | collective-permute-start | bytes 786440 | tf_op jit(solution)/shard_map/ppermute | solution.py:28
  9.0 12.1 %collective-permute-start.4 = (bf16[8,128,128]{2,1,0:T(8,128)(2,1)S(1)}, bf16[8,128,128]{2,1,0:T(8,128)(2,1)S(1)}, u32[]{:S(2)}, u32[]{:S(2)}) collective-permute-start(bf16[8,128,128]{2,1,0:T(8,128)(2,1)S(1)} %collective-permute-done.3.refs_7_), channel_id=1, source_target_pairs={{0,1},{1,0},{2,3},{3,2},{4,5},{5,4},{6,7},{7,6},{8,9},{9,8},{10,11... | collective-permute-start | bytes 786440 | tf_op jit(solution)/shard_map/ppermute | solution.py:28
  9.0 4.0 %collective-permute-start.6 = (bf16[8,8,128]{2,1,0:T(8,128)(2,1)}, bf16[8,8,128]{2,1,0:T(8,128)(2,1)S(1)}, u32[]{:S(2)}, u32[]{:S(2)}) collective-permute-start(bf16[8,8,128]{2,1,0:T(8,128)(2,1)} %refs_9_.1), channel_id=1, source_target_pairs={{0,2},{1,3},{2,0},{3,1},{4,6},{5,7},{6,4},{7,5},{8,10},{9,11},{10,... | collective-permute-start | bytes 49160 | tf_op jit(solution)/shard_map/ppermute | solution.py:28
  9.5 11.5 %collective-permute-start.5 = (bf16[8,8,128]{2,1,0:T(8,128)(2,1)}, bf16[8,8,128]{2,1,0:T(8,128)(2,1)S(1)}, u32[]{:S(2)}, u32[]{:S(2)}) collective-permute-start(bf16[8,8,128]{2,1,0:T(8,128)(2,1)} %refs_9_.1), channel_id=1, source_target_pairs={{0,1},{1,0},{2,3},{3,2},{4,5},{5,4},{6,7},{7,6},{8,9},{9,8},{10,11... | collective-permute-start | bytes 49160 | tf_op jit(solution)/shard_map/ppermute | solution.py:28
  12.9 5.2 %collective-permute-start = (bf16[128,128]{1,0:T(8,128)(2,1)S(1)}, bf16[128,128]{1,0:T(8,128)(2,1)S(1)}, u32[]{:S(2)}, u32[]{:S(2)}) collective-permute-start(bf16[128,128]{1,0:T(8,128)(2,1)S(1)} %get-tuple-element.20), channel_id=1, source_target_pairs={{0,1},{1,2},{2,3},{4,5},{5,6},{6,7},{8,9},{9,10},{10,11},{12,13},{... | collective-permute-start | bytes 98312 | tf_op jit(solution)/shard_map/ppermute | solution.py:24
  14.9 6.2 %collective-permute-start.7 = (bf16[8,8,128]{2,1,0:T(8,128)(2,1)S(1)}, bf16[8,8,128]{2,1,0:T(8,128)(2,1)S(1)}, u32[]{:S(2)}, u32[]{:S(2)}) collective-permute-start(bf16[8,8,128]{2,1,0:T(8,128)(2,1)S(1)} %collective-permute-done.6.refs_11_), channel_id=1, source_target_pairs={{0,1},{1,0},{2,3},{3,2},{4,5},{5,4},{6,7},{7,6},{8,9},{9,8},{10,11... | collective-permute-start | bytes 49160 | tf_op jit(solution)/shard_map/ppermute | solution.py:28
  18.1 1.0 %copy-start = (bf16[128,2048]{1,0:T(8,128)(2,1)S(1)}, bf16[128,2048]{1,0:T(8,128)(2,1)}, u32[]{:S(2)}) copy-start(bf16[128,2048]{1,0:T(8,128)(2,1)} %active_ref.3) | copy-start | bytes 1572868
  19.2 1.9 %copy-start.2 = (bf16[8,128,128]{2,1,0:T(8,128)(2,1)S(1)}, bf16[8,128,128]{2,1,0:T(8,128)(2,1)}, u32[]{:S(2)}) copy-start(bf16[8,128,128]{2,1,0:T(8,128)(2,1)} %refs_5_.1) | copy-start | bytes 786436
  19.2 1.9 %copy-start.3 = (bf16[8,8,128]{2,1,0:T(8,128)(2,1)S(1)}, bf16[8,8,128]{2,1,0:T(8,128)(2,1)}, u32[]{:S(2)}) copy-start(bf16[8,8,128]{2,1,0:T(8,128)(2,1)} %refs_9_.1) | copy-start | bytes 49156
  19.2 1.9 %copy-start.4 = (bf16[128,2048]{1,0:T(8,128)(2,1)S(1)}, bf16[128,2048]{1,0:T(8,128)(2,1)}, u32[]{:S(2)}) copy-start(bf16[128,2048]{1,0:T(8,128)(2,1)} %refs_1_.1) | copy-start | bytes 1572868
  19.2 1.9 %copy-start.5 = (bf16[8,2048]{1,0:T(8,128)(2,1)S(1)}, bf16[8,2048]{1,0:T(8,128)(2,1)}, u32[]{:S(2)}) copy-start(bf16[8,2048]{1,0:T(8,128)(2,1)} %refs_3_.1) | copy-start | bytes 98308
  35.0 21.8 %collective-permute-start.8 = (f32[2,8,136,128]{3,2,1,0:T(8,128)S(1)}, f32[2,8,136,128]{3,2,1,0:T(8,128)}, u32[]{:S(2)}, u32[]{:S(2)}) collective-permute-start(f32[2,8,136,128]{3,2,1,0:T(8,128)S(1)} %get-tuple-element.13), channel_id=1, source_target_pairs={{0,1},{1,0},{2,3},{3,2},{4,5},{5,4},{6,7},{7,6},{8,9},{9,8},{10,11... | collective-permute-start | bytes 3342344 | tf_op jit(solution)/shard_map/ppermute | solution.py:28
  35.1 6.1 %collective-permute-start.10 = (bf16[16,32,128]{2,1,0:T(8,128)(2,1)S(1)}, bf16[16,32,128]{2,1,0:T(8,128)(2,1)S(1)}, u32[]{:S(2)}, u32[]{:S(2)}) collective-permute-start(bf16[16,32,128]{2,1,0:T(8,128)(2,1)S(1)} %get-tuple-element.16), channel_id=1, source_target_pairs={{0,4},{4,8},{8,12},{12,0},{16,20},{20,24},{24,28},{28,16},{32,36},... | collective-permute-start | bytes 393224 | tf_op jit(solution)/shard_map/ppermute | solution.py:33
  36.9 7.9 %collective-permute-start.11 = (bf16[16,32,128]{2,1,0:T(8,128)(2,1)S(1)}, bf16[16,32,128]{2,1,0:T(8,128)(2,1)S(1)}, u32[]{:S(2)}, u32[]{:S(2)}) collective-permute-start(bf16[16,32,128]{2,1,0:T(8,128)(2,1)S(1)} %get-tuple-element.17), channel_id=1, source_target_pairs={{0,8},{4,12},{8,0},{12,4},{16,24},{20,28},{24,16},{28,20},{32,40},... | collective-permute-start | bytes 393224 | tf_op jit(solution)/shard_map/ppermute | solution.py:33
  37.8 8.0 %collective-permute-start.12 = (bf16[16,32,128]{2,1,0:T(8,128)(2,1)S(1)}, bf16[16,32,128]{2,1,0:T(8,128)(2,1)S(1)}, u32[]{:S(2)}, u32[]{:S(2)}) collective-permute-start(bf16[16,32,128]{2,1,0:T(8,128)(2,1)S(1)} %get-tuple-element.18), channel_id=1, source_target_pairs={{0,12},{4,0},{8,4},{12,8},{16,28},{20,16},{24,20},{28,24},{32,44},... | collective-permute-start | bytes 393224 | tf_op jit(solution)/shard_map/ppermute | solution.py:33
  46.5 21.5 %copy-start.1 = (bf16[128,2048]{1,0:T(8,128)(2,1)S(1)}, bf16[128,2048]{1,0:T(8,128)(2,1)}, u32[]{:S(2)}) copy-start(bf16[128,2048]{1,0:T(8,128)(2,1)} %active_ref.3) | copy-start | bytes 1572868
  46.5 21.5 %all-to-all-start = ((bf16[16,32,128]{2,1,0:T(8,128)(2,1)}), bf16[16,32,128]{2,1,0:T(8,128)(2,1)S(1)}, u32[]{:S(2)}, u32[]{:S(2)}) async-start(bf16[16,32,128]{2,1,0:T(8,128)(2,1)} %shard_map.79), calls=%async_computation | async-start | bytes 262144 | tf_op jit(solution)/shard_map/all_to_all | solution.py:38
  57.9 34.2 %collective-permute-start.9 = (f32[8,136,128]{2,1,0:T(8,128)S(1)}, f32[8,136,128]{2,1,0:T(8,128)S(1)}, u32[]{:S(2)}, u32[]{:S(2)}) collective-permute-start(f32[8,136,128]{2,1,0:T(8,128)S(1)} %fusion), channel_id=1, source_target_pairs={{0,2},{1,3},{2,0},{3,1},{4,6},{5,7},{6,4},{7,5},{8,10},{9,11},{10,... | collective-permute-start | bytes 1671176 | tf_op jit(solution)/shard_map/ppermute | solution.py:28
  81.9 5.0 %collective-permute-start.13 = (bf16[32,2048]{1,0:T(8,128)(2,1)S(1)}, bf16[32,2048]{1,0:T(8,128)(2,1)S(1)}, u32[]{:S(2)}, u32[]{:S(2)}) collective-permute-start(bf16[32,2048]{1,0:T(8,128)(2,1)S(1)} %shard_map.81.refs_0_), channel_id=1, source_target_pairs={{0,4},{4,8},{8,12},{12,0},{16,20},{20,24},{24,28},{28,16},{32,36},... | collective-permute-start | bytes 393224 | tf_op jit(solution)/shard_map/ppermute | solution.py:33
  83.4 6.6 %collective-permute-start.14 = (bf16[32,2048]{1,0:T(8,128)(2,1)S(1)}, bf16[32,2048]{1,0:T(8,128)(2,1)S(1)}, u32[]{:S(2)}, u32[]{:S(2)}) collective-permute-start(bf16[32,2048]{1,0:T(8,128)(2,1)S(1)} %shard_map.81.refs_0_), channel_id=1, source_target_pairs={{0,8},{4,12},{8,0},{12,4},{16,24},{20,28},{24,16},{28,20},{32,40},... | collective-permute-start | bytes 393224 | tf_op jit(solution)/shard_map/ppermute | solution.py:33
  85.0 6.3 %collective-permute-start.15 = (bf16[32,2048]{1,0:T(8,128)(2,1)S(1)}, bf16[32,2048]{1,0:T(8,128)(2,1)S(1)}, u32[]{:S(2)}, u32[]{:S(2)}) collective-permute-start(bf16[32,2048]{1,0:T(8,128)(2,1)S(1)} %shard_map.81.refs_0_), channel_id=1, source_target_pairs={{0,12},{4,0},{8,4},{12,8},{16,28},{20,16},{24,20},{28,24},{32,44},... | collective-permute-start | bytes 393224 | tf_op jit(solution)/shard_map/ppermute | solution.py:33
